TPU v7x, 32 devices: a whole 2x2x4 slice. The times are simulated.
32 devices in a mesh: leaf: 32 (over z, y, x, core).
Axes of the slice: x: 2, y: 2, z: 4, core: 2. Of those that a mesh axis runs over, the one named last changes fastest.
Arguments:
- points: bfloat16 [49152, 128], P('leaf'), may hold values from -20 to 20
- weights: bfloat16 [49152, 256], P('leaf'), may hold values from -4 to 4
- targets: bfloat16 [49152, 256], P('leaf'), may hold values from -4 to 4
- near_mask: int32 [32, 4], P('leaf'), may hold values from 0 to 1, as said below
- leaf_skeleton: int32 [32, 256], P('leaf'), may hold values from 0 to 1535, as said below
- node_skeleton: int32 [4, 32, 256], P(None, 'leaf'), may hold values from 0 to 511, as said below
Outputs:
- updated: bfloat16 [49152, 256], P('leaf')
- residual: float32 [49152, 256], P('leaf')
Inputs may be any that keep to these rules, and one draw needn't show every extreme that they name: near_mask is 0 where the listed leaf would lie outside the tree; leaf i lists leaf j exactly when leaf j lists leaf i; the number of listed leaves differs from leaf to leaf. `leaf_skeleton`: row i holds 256 distinct increasing point numbers counted within leaf i. `node_skeleton`: entry [l, i] holds 256 distinct increasing positions in the union of the two children's skeletons of the level l + 1 node containing leaf i; equal for all leaves of that node.
All inputs are finite; a program needn't handle non-finite values.
Results may differ from a plain program's by a relative error of at most 0.0034.
Values may be sent and summed in bfloat16 or wider, within the bound.
A program may use at most 64 MiB of HBM per device.

v0:
```python
import functools

import jax
import jax.numpy as jnp
from jax import lax
from jax.experimental import pallas as pl
from jax.experimental.pallas import tpu as pltpu
from jax.sharding import PartitionSpec as P

LEVELS = 5

ridge_weight = 1.0
damping = 0.25
LOG2E = 1.4426950408889634

CHUNK = 256
BLOCK = 256


def pieces(rows):
    wide = rows.astype(jnp.float32)
    sq = jnp.sum(wide * wide, axis=1, keepdims=True)
    hi = sq.astype(jnp.bfloat16).astype(jnp.float32)
    rest = sq - hi
    mid = rest.astype(jnp.bfloat16).astype(jnp.float32)
    return hi, mid, rest - mid


def extra(rows, parts, first, second):
    hi, mid, low = parts
    lane = lax.broadcasted_iota(jnp.int32, rows.shape, 1)

    def picked(which, start):
        if which is None:
            return jnp.where((lane >= start) & (lane < start + 3), 1.0, 0.0)
        zero = jnp.zeros(rows.shape, jnp.float32)
        out = jnp.where(lane == start, hi, zero)
        out = jnp.where(lane == start + 1, mid, out)
        return jnp.where(lane == start + 2, low, out)

    return picked(first, 0) + picked(second, 3)


def left_form(rows, parts):
    tail = -extra(rows, parts, "norms", None)
    return jnp.concatenate(
        [(rows.astype(jnp.float32) * 2.0).astype(jnp.bfloat16), tail.astype(jnp.bfloat16)], axis=1
    )


def right_form(rows, parts):
    tail = extra(rows, parts, None, "norms")
    return jnp.concatenate([rows, tail.astype(jnp.bfloat16)], axis=1)


def affinity(left, right, features):
    s = lax.dot_general(left, right, (((1,), (1,)), ((), ())), preferred_element_type=jnp.float32)
    return jnp.exp2(s * (LOG2E / features))


def dot(a, b):
    return jnp.dot(a, b, preferred_element_type=jnp.float32)


def step(
    n,
    mask_ref,
    points_ref,
    weights_ref,
    targets_ref,
    index_ref,
    updated_ref,
    residual_ref,
    near_x,
    near_w,
    sib_x,
    sib_w,
    q_x,
    q_w,
    union,
    own_left,
    own_right,
    other_right,
    total,
    x_send,
    x_recv,
    r_send,
    r_recv,
    s_send,
    s_recv,
    q_send,
    q_recv,
    l_send,
    l_recv,
):
    me = lax.axis_index("leaf")
    rows, features = points_ref.shape
    skel = index_ref.shape[0]
    chunks = rows // CHUNK
    per_half = chunks // 2
    half = rows // 2
    core = lax.rem(me, 2)
    side = lax.rem(me // 2, 2)
    flip = core + side - 2 * core * side
    relay_to = me + 4 - 8 * side
    relay_from = me - 4 + 8 * side
    gives = (relay_to >= 0) & (relay_to < n)
    takes = (relay_from >= 0) & (relay_from < n)

    def bit(level):
        return lax.rem(me // (2**level), 2)

    def across(level):
        return me + (1 - 2 * bit(level)) * (2**level)

    barrier = pltpu.get_barrier_semaphore()
    for level in range(LEVELS):
        pl.semaphore_signal(barrier, inc=1, device_id=(across(level),), device_id_type=pl.DeviceIdType.MESH)

    @pl.when(gives)
    def _():
        pl.semaphore_signal(barrier, inc=1, device_id=(relay_to,), device_id_type=pl.DeviceIdType.MESH)

    @pl.when(takes)
    def _():
        pl.semaphore_signal(barrier, inc=1, device_id=(relay_from,), device_id_type=pl.DeviceIdType.MESH)

    pl.semaphore_wait(barrier, LEVELS + gives.astype(jnp.int32) + takes.astype(jnp.int32))

    def remote(src, dst, send, recv, device):
        return pltpu.make_async_remote_copy(
            src_ref=src, dst_ref=dst, send_sem=send, recv_sem=recv,
            device_id=(device,), device_id_type=pl.DeviceIdType.MESH,
        )

    def x_copies(k):
        part = pl.ds(k * CHUNK, CHUNK)
        return [
            remote(points_ref.at[part], near_x.at[0, part], x_send.at[k, 0], x_recv.at[k, 0], across(1)),
            remote(weights_ref.at[part], near_w.at[0, part], x_send.at[k, 1], x_recv.at[k, 1], across(1)),
        ]

    def r_copies(k):
        part = pl.ds(k * CHUNK, CHUNK)
        return [
            remote(near_x.at[0, part], near_x.at[1, part], r_send.at[k, 0], r_recv.at[k, 0], relay_to),
            remote(near_w.at[0, part], near_w.at[1, part], r_send.at[k, 1], r_recv.at[k, 1], relay_to),
        ]

    def q_copies(h, slot):
        part = pl.ds(h * half, half)
        return [
            remote(near_x.at[slot, part], q_x.at[part], q_send.at[h, 0], q_recv.at[h, 0], across(0)),
            remote(near_w.at[slot, part], q_w.at[part], q_send.at[h, 1], q_recv.at[h, 1], across(0)),
        ]

    def s_copies():
        return [
            remote(points_ref, sib_x, s_send.at[0], s_recv.at[0], across(0)),
            remote(weights_ref, sib_w, s_send.at[1], s_recv.at[1], across(0)),
        ]

    def l_copy(level):
        mine = union.at[level, bit(level)]
        return remote(mine, mine, l_send.at[level], l_recv.at[level], across(level))

    def start(copies):
        for copy in copies:
            copy.start()

    def landed(copies):
        for copy in copies:
            copy.wait_recv()

    def left_behind(copies):
        for copy in copies:
            copy.wait_send()

    def x_landed(k):
        landed(x_copies(k))

        @pl.when(gives)
        def _():
            start(r_copies(k))

    def near_unit(x_ref, w_ref, h, scale, own=False):
        part = slice(h * half, (h + 1) * half)
        if not own:
            x = x_ref[part, :]
            other_right[...] = right_form(x, pieces(x))

        def body(r, _):
            at = pl.ds(pl.multiple_of(r * BLOCK, BLOCK), BLOCK)
            right = own_right[part, :] if own else other_right[...]
            tile = affinity(own_left[at, :], right, features).astype(jnp.bfloat16)
            value = dot(tile, w_ref[part, :])
            if scale is not None:
                value = value * scale
            total[at, :] += value
            return 0

        lax.fori_loop(0, rows // BLOCK, body, 0)

    def far_unit(level):
        pair = union[level, 1 - bit(level)]
        p = pair[:, :features]
        other_right[:skel, :] = right_form(p, pieces(p))

        def body(r, _):
            at = pl.ds(pl.multiple_of(r * BLOCK, BLOCK), BLOCK)
            tile = affinity(own_left[at, :], other_right[:skel, :], features).astype(jnp.bfloat16)
            total[at, :] += dot(tile, union[level, 1 - bit(level), :, features:])
            return 0

        lax.fori_loop(0, rows // BLOCK, body, 0)

    def chosen(level, count):
        col = lax.broadcasted_iota(jnp.int32, (skel, count), 1)
        return jnp.where(col == index_ref[:, level : level + 1], 1.0, 0.0).astype(jnp.bfloat16)

    def climb(level):
        landed([l_copy(level)])
        low, high = union[level, 0], union[level, 1]
        p = jnp.concatenate([low[:, :features], high[:, :features]], axis=0)
        q = jnp.concatenate([low[:, features:], high[:, features:]], axis=0)
        sk = dot(chosen(level + 1, 2 * skel), p).astype(jnp.bfloat16)
        aff = affinity(left_form(sk, pieces(sk)), right_form(p, pieces(p)), features)
        share = (aff / jnp.sum(aff, axis=0, keepdims=True)).astype(jnp.bfloat16)
        union[level + 1, bit(level + 1), :, :features] = sk
        union[level + 1, bit(level + 1), :, features:] = dot(share, q).astype(jnp.bfloat16)
        l_copy(level + 1).start()

    def listed(column):
        return mask_ref[0, column].astype(jnp.float32)

    start(x_copies(0) + s_copies() + x_copies(1))

    x = points_ref[...]
    norms = pieces(x)
    own_right[...] = right_form(x, norms)
    sk = dot(chosen(0, rows), x).astype(jnp.bfloat16)
    tile = affinity(left_form(sk, pieces(sk)), own_right[...], features).astype(jnp.bfloat16)
    union[0, core, :, :features] = sk
    union[0, core, :, features:] = dot(tile, weights_ref[...]).astype(jnp.bfloat16)
    l_copy(0).start()
    own_left[...] = left_form(x, norms)
    total[...] = jnp.zeros_like(total)

    climb(0)
    for k in range(2, chunks):
        start(x_copies(k))
    near_unit(points_ref, weights_ref, 0, None, own=True)
    x_landed(0)
    far_unit(0)
    climb(1)
    near_unit(points_ref, weights_ref, 1, None, own=True)
    x_landed(1)
    far_unit(1)
    climb(2)
    landed(s_copies())
    near_unit(sib_x, sib_w, 0, listed(2 * core))
    far_unit(2)
    for k in range(2, per_half):
        x_landed(k)
    climb(3)
    near_unit(sib_x, sib_w, 1, listed(2 * core))
    far_unit(3)

    @pl.when(flip == 0)
    def _():
        start(q_copies(0, 0))

    near_unit(near_x.at[0], near_w.at[0], 0, listed(1 + 2 * side))
    x_landed(per_half)
    landed([l_copy(LEVELS - 1)])
    far_unit(LEVELS - 1)
    for k in range(per_half + 1, chunks - 1):
        x_landed(k)

    @pl.when(takes)
    def _():
        for k in range(per_half):
            landed(r_copies(k))

        @pl.when(flip == 1)
        def _():
            start(q_copies(0, 1))

        near_unit(near_x.at[1], near_w.at[1], 0, listed(3 - 2 * side))

    x_landed(chunks - 1)

    @pl.when(flip == 0)
    def _():
        start(q_copies(1, 0))

    near_unit(near_x.at[0], near_w.at[0], 1, listed(1 + 2 * side))

    takes_q = (flip == 1) | takes

    @pl.when(takes_q)
    def _():
        landed(q_copies(0, 0))
        near_unit(q_x, q_w, 0, listed(2 - 2 * core))

    @pl.when(takes)
    def _():
        for k in range(per_half, chunks):
            landed(r_copies(k))

        @pl.when(flip == 1)
        def _():
            start(q_copies(1, 1))

        near_unit(near_x.at[1], near_w.at[1], 1, listed(3 - 2 * side))

    @pl.when(takes_q)
    def _():
        landed(q_copies(1, 0))
        near_unit(q_x, q_w, 1, listed(2 - 2 * core))

    def finish(r, _):
        at = pl.ds(pl.multiple_of(r * BLOCK, BLOCK), BLOCK)
        w = weights_ref[at, :].astype(jnp.float32)
        res = targets_ref[at, :].astype(jnp.float32) - ridge_weight * w - total[at, :]
        residual_ref[at, :] = res
        updated_ref[at, :] = (w + damping * res / (1.0 + ridge_weight)).astype(jnp.bfloat16)
        return 0

    lax.fori_loop(0, rows // BLOCK, finish, 0)

    left_behind(s_copies())
    for k in range(chunks):
        left_behind(x_copies(k))
    for level in range(LEVELS):
        left_behind([l_copy(level)])

    @pl.when(gives)
    def _():
        for k in range(chunks):
            left_behind(r_copies(k))

    @pl.when((flip == 0) | takes)
    def _():
        for h in range(2):
            left_behind(q_copies(h, 0))


def local(n, points, weights, targets, near_mask, leaf_skeleton, node_skeleton):
    rows, features = points.shape
    rhs = weights.shape[1]
    skel = leaf_skeleton.shape[1]
    chunks = rows // CHUNK
    index = jnp.concatenate([leaf_skeleton, node_skeleton[:, 0]], axis=0).T
    vmem = pl.BlockSpec(memory_space=pltpu.VMEM)
    dma = pltpu.SemaphoreType.DMA
    bf16 = jnp.bfloat16
    return pl.pallas_call(
        functools.partial(step, n),
        out_shape=(
            jax.ShapeDtypeStruct((rows, rhs), bf16),
            jax.ShapeDtypeStruct((rows, rhs), jnp.float32),
        ),
        in_specs=[pl.BlockSpec(memory_space=pltpu.SMEM)] + [vmem] * 4,
        out_specs=(vmem, vmem),
        scratch_shapes=[
            pltpu.VMEM((2, rows, features), bf16),
            pltpu.VMEM((2, rows, rhs), bf16),
            pltpu.VMEM((rows, features), bf16),
            pltpu.VMEM((rows, rhs), bf16),
            pltpu.VMEM((rows, features), bf16),
            pltpu.VMEM((rows, rhs), bf16),
            pltpu.VMEM((LEVELS, 2, skel, features + rhs), bf16),
            pltpu.VMEM((rows, 2 * features), bf16),
            pltpu.VMEM((rows, 2 * features), bf16),
            pltpu.VMEM((rows // 2, 2 * features), bf16),
            pltpu.VMEM((rows, rhs), jnp.float32),
            dma((chunks, 2)),
            dma((chunks, 2)),
            dma((chunks, 2)),
            dma((chunks, 2)),
            dma((2,)),
            dma((2,)),
            dma((2, 2)),
            dma((2, 2)),
            dma((LEVELS,)),
            dma((LEVELS,)),
        ],
        compiler_params=pltpu.CompilerParams(
            collective_id=0, has_side_effects=True, vmem_limit_bytes=60 * 1024 * 1024
        ),
    )(near_mask, points, weights, targets, index)


def solution(mesh):
    placed = (
        P("leaf", None),
        P("leaf", None),
        P("leaf", None),
        P("leaf", None),
        P("leaf", None),
        P(None, "leaf", None),
    )
    return jax.shard_map(
        functools.partial(local, mesh.shape["leaf"]),
        mesh=mesh,
        in_specs=placed,
        out_specs=(P("leaf", None), P("leaf", None)),
        check_vma=False,
    )
```

profile of v0, /device:TPU:2, one launch (start us, length us, event | category | flops | bytes accessed | tf_op | source)
XLA Modules:
  0.0 74.3 jit_solution(18116530026395321066)
XLA Ops:
  0.6 0.7 copy.13
  1.3 0.7 pad_add_fusion
  2.0 0.8 %copy.10 = s32[5,256]{0,1:T(8,128)} copy(s32[5,256]{1,0:T(8,128)S(1)} %pad_add_fusion) | data formatting | bytes 10240 | tf_op jit(solution)/shard_map/concatenate | solution.py:354
  2.8 68.1 %shard_map.77 = (bf16[1536,256]{1,0:T(8,128)(2,1)}, f32[1536,256]{1,0:T(8,128)}) custom-call(s32[1,4]{1,0:T(1,128)} %mask_ref.1, bf16[1536,128]{1,0:T(8,128)(2,1)} %points_ref.1, bf16[1536,256]{1,0:T(8,128)(2,1)} %weights_ref.1, bf16[1536,256]{1,0:T(8,128)(2,1)} %targets_ref.1, s32[256,5]{1,0:T(8,128)} %bitcast.4), custom_call_target="tpu_custom_call" | custom-call | tf_op jit(solution)/shard_map/pallas_call | solution.py:358
  70.9 0.0 copy-start
  70.9 2.2 %copy.16 = bf16[1536,256]{1,0:T(8,128)(2,1)} copy(bf16[1536,256]{1,0:T(8,128)(2,1)} %get-tuple-element.4) | data formatting | bytes 1572864
  73.1 0.0 copy-done
  73.1 1.1 %copy.17 = f32[1536,256]{1,0:T(8,128)} copy(f32[1536,256]{1,0:T(8,128)S(1)} %copy-done) | data formatting | bytes 3145728
Async XLA Ops:
  70.9 2.2 %copy-start = (f32[1536,256]{1,0:T(8,128)S(1)}, f32[1536,256]{1,0:T(8,128)}, u32[]{:S(2)}) copy-start(f32[1536,256]{1,0:T(8,128)} %get-tuple-element.5) | copy-start | bytes 4718596
where the time goes:
time: 74.5 us; the launch traced here: 74.3 us
  Pallas kernels  68.1 us (91%)
  local copies, waits for them, and re-layouts  4.82 us (6%)
    pallas_call x1, Pallas kernels, local(): pl.pallas_call(functools.partial(step, n), out_shape=(jax.ShapeDtypeStruc...  68.1 us
    unnamed x5, local copies, waits for them, and re-layouts  4.02 us

commit v1 on v0

--- a/solution.py
+++ b/solution.py
@@ -14,7 +14,7 @@
 LOG2E = 1.4426950408889634
 
 CHUNK = 256
-BLOCK = 256
+BLOCK = 768
 
 
 def pieces(rows):
@@ -67,10 +67,9 @@
     mask_ref,
     points_ref,
     weights_ref,
-    targets_ref,
-    index_ref,
-    updated_ref,
-    residual_ref,
+    leaf_index_ref,
+    node_index_ref,
+    total,
     near_x,
     near_w,
     sib_x,
@@ -81,7 +80,8 @@
     own_left,
     own_right,
     other_right,
-    total,
+    other_w,
+    indices,
     x_send,
     x_recv,
     r_send,
@@ -95,7 +95,7 @@
 ):
     me = lax.axis_index("leaf")
     rows, features = points_ref.shape
-    skel = index_ref.shape[0]
+    skel = leaf_index_ref.shape[1]
     chunks = rows // CHUNK
     per_half = chunks // 2
     half = rows // 2
@@ -201,22 +201,26 @@
 
         lax.fori_loop(0, rows // BLOCK, body, 0)
 
-    def far_unit(level):
-        pair = union[level, 1 - bit(level)]
-        p = pair[:, :features]
-        other_right[:skel, :] = right_form(p, pieces(p))
+    def far_unit(levels):
+        depth = len(levels) * skel
+        for i, level in enumerate(levels):
+            part = slice(i * skel, (i + 1) * skel)
+            pair = union[level, 1 - bit(level)]
+            p = pair[:, :features]
+            other_right[part, :] = right_form(p, pieces(p))
+            other_w[part, :] = pair[:, features:]
 
         def body(r, _):
             at = pl.ds(pl.multiple_of(r * BLOCK, BLOCK), BLOCK)
-            tile = affinity(own_left[at, :], other_right[:skel, :], features).astype(jnp.bfloat16)
-            total[at, :] += dot(tile, union[level, 1 - bit(level), :, features:])
+            tile = affinity(own_left[at, :], other_right[:depth, :], features).astype(jnp.bfloat16)
+            total[at, :] += dot(tile, other_w[:depth, :])
             return 0
 
         lax.fori_loop(0, rows // BLOCK, body, 0)
 
     def chosen(level, count):
-        col = lax.broadcasted_iota(jnp.int32, (skel, count), 1)
-        return jnp.where(col == index_ref[:, level : level + 1], 1.0, 0.0).astype(jnp.bfloat16)
+        col = lax.broadcasted_iota(jnp.int32, (skel, count), 1).astype(jnp.float32)
+        return jnp.where(col == indices[:, level : level + 1], 1.0, 0.0).astype(jnp.bfloat16)
 
     def climb(level):
         landed([l_copy(level)])
@@ -235,6 +239,10 @@
 
     start(x_copies(0) + s_copies() + x_copies(1))
 
+    table = [leaf_index_ref[...]] + [node_index_ref[level] for level in range(LEVELS - 1)]
+    table = jnp.concatenate(table + [table[0]] * (8 - LEVELS), axis=0)
+    indices[...] = table.astype(jnp.float32).T
+
     x = points_ref[...]
     norms = pieces(x)
     own_right[...] = right_form(x, norms)
@@ -251,29 +259,25 @@
         start(x_copies(k))
     near_unit(points_ref, weights_ref, 0, None, own=True)
     x_landed(0)
-    far_unit(0)
+    near_unit(points_ref, weights_ref, 1, None, own=True)
     climb(1)
-    near_unit(points_ref, weights_ref, 1, None, own=True)
     x_landed(1)
-    far_unit(1)
-    climb(2)
     landed(s_copies())
     near_unit(sib_x, sib_w, 0, listed(2 * core))
-    far_unit(2)
+    climb(2)
+    near_unit(sib_x, sib_w, 1, listed(2 * core))
     for k in range(2, per_half):
         x_landed(k)
+
+    @pl.when(flip == 0)
+    def _():
+        start(q_copies(0, 0))
+
     climb(3)
-    near_unit(sib_x, sib_w, 1, listed(2 * core))
-    far_unit(3)
-
-    @pl.when(flip == 0)
-    def _():
-        start(q_copies(0, 0))
-
     near_unit(near_x.at[0], near_w.at[0], 0, listed(1 + 2 * side))
     x_landed(per_half)
-    landed([l_copy(LEVELS - 1)])
-    far_unit(LEVELS - 1)
+    far_unit([0, 1, 2])
+
     for k in range(per_half + 1, chunks - 1):
         x_landed(k)
 
@@ -303,6 +307,9 @@
         landed(q_copies(0, 0))
         near_unit(q_x, q_w, 0, listed(2 - 2 * core))
 
+    landed([l_copy(LEVELS - 1)])
+    far_unit([3, 4])
+
     @pl.when(takes)
     def _():
         for k in range(per_half, chunks):
@@ -318,16 +325,6 @@
     def _():
         landed(q_copies(1, 0))
         near_unit(q_x, q_w, 1, listed(2 - 2 * core))
-
-    def finish(r, _):
-        at = pl.ds(pl.multiple_of(r * BLOCK, BLOCK), BLOCK)
-        w = weights_ref[at, :].astype(jnp.float32)
-        res = targets_ref[at, :].astype(jnp.float32) - ridge_weight * w - total[at, :]
-        residual_ref[at, :] = res
-        updated_ref[at, :] = (w + damping * res / (1.0 + ridge_weight)).astype(jnp.bfloat16)
-        return 0
-
-    lax.fori_loop(0, rows // BLOCK, finish, 0)
 
     left_behind(s_copies())
     for k in range(chunks):
@@ -351,18 +348,14 @@
     rhs = weights.shape[1]
     skel = leaf_skeleton.shape[1]
     chunks = rows // CHUNK
-    index = jnp.concatenate([leaf_skeleton, node_skeleton[:, 0]], axis=0).T
     vmem = pl.BlockSpec(memory_space=pltpu.VMEM)
     dma = pltpu.SemaphoreType.DMA
     bf16 = jnp.bfloat16
-    return pl.pallas_call(
+    total = pl.pallas_call(
         functools.partial(step, n),
-        out_shape=(
-            jax.ShapeDtypeStruct((rows, rhs), bf16),
-            jax.ShapeDtypeStruct((rows, rhs), jnp.float32),
-        ),
+        out_shape=jax.ShapeDtypeStruct((rows, rhs), jnp.float32),
         in_specs=[pl.BlockSpec(memory_space=pltpu.SMEM)] + [vmem] * 4,
-        out_specs=(vmem, vmem),
+        out_specs=vmem,
         scratch_shapes=[
             pltpu.VMEM((2, rows, features), bf16),
             pltpu.VMEM((2, rows, rhs), bf16),
@@ -374,7 +367,8 @@
             pltpu.VMEM((rows, 2 * features), bf16),
             pltpu.VMEM((rows, 2 * features), bf16),
             pltpu.VMEM((rows // 2, 2 * features), bf16),
-            pltpu.VMEM((rows, rhs), jnp.float32),
+            pltpu.VMEM((rows // 2, rhs), bf16),
+            pltpu.VMEM((skel, 8), jnp.float32),
             dma((chunks, 2)),
             dma((chunks, 2)),
             dma((chunks, 2)),
@@ -389,7 +383,11 @@
         compiler_params=pltpu.CompilerParams(
             collective_id=0, has_side_effects=True, vmem_limit_bytes=60 * 1024 * 1024
         ),
-    )(near_mask, points, weights, targets, index)
+    )(near_mask, points, weights, leaf_skeleton, node_skeleton)
+    wide = weights.astype(jnp.float32)
+    residual = targets.astype(jnp.float32) - ridge_weight * wide - total
+    updated = (wide + damping * residual / (1.0 + ridge_weight)).astype(jnp.bfloat16)
+    return updated, residual
 
 
 def solution(mesh):

time: 74.5 us -> 66.5 us (0.89)
  Pallas kernels: 68.1 us -> 62.4 us
  local copies, waits for them, and re-layouts: 4.82 us -> 0.01 us
  other arithmetic: 0.69 us -> 3.15 us
    pallas_call x1, Pallas kernels: 68.1 us -> 62.4 us  [local(): pl.pallas_call(functools.partial(step, n), out_shape=jax.ShapeDtypeStruct...]
    unnamed x5 -> x4, local copies, waits for them, and re-layouts: 4.02 us -> 0.01 us
    convert_element_type x0 -> x1, other arithmetic: none -> 3.15 us  [local(): (wide + damping * residual / (1.0 + ridge_weight)).astype(jnp.bfloat16)]
    concatenate x1 -> x0, local copies, waits for them, and re-layouts: 0.8 us -> none  [local(): index = jnp.concatenate([leaf_skeleton, node_skeleton[:, 0]], axis=0).T]
where the time goes in v1:
time: 66.5 us; the launch traced here: 66.3 us
  Pallas kernels  62.4 us (94%)
  other arithmetic  3.15 us (5%)
  between operations  0.67 us (1%)
    pallas_call x1, Pallas kernels, local(): pl.pallas_call(functools.partial(step, n), out_shape=jax.ShapeDtypeStruct...  62.4 us
    convert_element_type x1, other arithmetic, local(): (wide + damping * residual / (1.0 + ridge_weight)).astype(jnp.bfloat16)  3.15 us

profile of v1, /device:TPU:2, one launch (start us, length us, event | category | flops | bytes accessed | tf_op | source)
XLA Modules:
  0.0 66.3 jit_solution(6481274399763348670)
XLA Ops:
  0.6 0.0 copy-start
  0.6 0.0 copy-start.1
  0.7 62.4 %shard_map.77 = f32[1536,256]{1,0:T(8,128)} custom-call(s32[1,4]{1,0:T(1,128)} %mask_ref.1, bf16[1536,128]{1,0:T(8,128)(2,1)} %points_ref.1, bf16[1536,256]{1,0:T(8,128)(2,1)} %weights_ref.1, s32[1,256]{1,0:T(1,128)} %leaf_index_ref.1, s32[4,1,256]{2,1,0:T(1,128)} %node_index_ref.1), custom_call_target="tpu_custom_call" | custom-call | tf_op jit(solution)/shard_map/pallas_call | solution.py:354
  63.1 0.0 copy-done
  63.1 0.0 copy-done.1
  63.1 3.1 %fusion.1 = (bf16[1536,256]{1,0:T(8,128)(2,1)}, f32[1536,256]{1,0:T(8,128)}) fusion(bf16[1536,256]{1,0:T(8,128)(2,1)S(1)} %copy-done, f32[1536,256]{1,0:T(8,128)} %shard_map.77, bf16[1536,256]{1,0:T(8,128)(2,1)S(1)} %copy-done.1), kind=kLoop, calls=%fused_computation.3 | loop fusion | flops 2752512 | bytes 5505024 | tf_op jit(solution)/shard_map/convert_element_type | solution.py:389
Async XLA Ops:
  0.6 62.5 %copy-start = (bf16[1536,256]{1,0:T(8,128)(2,1)S(1)}, bf16[1536,256]{1,0:T(8,128)(2,1)}, u32[]{:S(2)}) copy-start(bf16[1536,256]{1,0:T(8,128)(2,1)} %weights_ref.1) | copy-start | bytes 2359300
  0.6 62.5 %copy-start.1 = (bf16[1536,256]{1,0:T(8,128)(2,1)S(1)}, bf16[1536,256]{1,0:T(8,128)(2,1)}, u32[]{:S(2)}) copy-start(bf16[1536,256]{1,0:T(8,128)(2,1)} %param.8) | copy-start | bytes 2359300

commit v2 on v1

--- a/solution.py
+++ b/solution.py
@@ -258,28 +258,35 @@
     for k in range(2, chunks):
         start(x_copies(k))
     near_unit(points_ref, weights_ref, 0, None, own=True)
-    x_landed(0)
+    for k in range(0, 1):
+        x_landed(k)
     near_unit(points_ref, weights_ref, 1, None, own=True)
+    for k in range(1, chunks // 3):
+        x_landed(k)
     climb(1)
-    x_landed(1)
     landed(s_copies())
     near_unit(sib_x, sib_w, 0, listed(2 * core))
+    for k in range(chunks // 3, per_half):
+        x_landed(k)
+    @pl.when(flip == 0)
+    def _():
+        start(q_copies(0, 0))
+
     climb(2)
     near_unit(sib_x, sib_w, 1, listed(2 * core))
-    for k in range(2, per_half):
-        x_landed(k)
-
+    for k in range(per_half, chunks * 2 // 3):
+        x_landed(k)
+    near_unit(near_x.at[0], near_w.at[0], 0, listed(1 + 2 * side))
+    climb(3)
+    for k in range(chunks * 2 // 3, chunks - 1):
+        x_landed(k)
+    far_unit([0, 1, 2])
+    for k in range(chunks - 1, chunks):
+        x_landed(k)
     @pl.when(flip == 0)
     def _():
-        start(q_copies(0, 0))
-
-    climb(3)
-    near_unit(near_x.at[0], near_w.at[0], 0, listed(1 + 2 * side))
-    x_landed(per_half)
-    far_unit([0, 1, 2])
-
-    for k in range(per_half + 1, chunks - 1):
-        x_landed(k)
+        start(q_copies(1, 0))
+
 
     @pl.when(takes)
     def _():
@@ -291,12 +298,6 @@
             start(q_copies(0, 1))
 
         near_unit(near_x.at[1], near_w.at[1], 0, listed(3 - 2 * side))
-
-    x_landed(chunks - 1)
-
-    @pl.when(flip == 0)
-    def _():
-        start(q_copies(1, 0))
 
     near_unit(near_x.at[0], near_w.at[0], 1, listed(1 + 2 * side))
 

time: 66.5 us -> 60.8 us (0.914)
  the two profiles are of different devices: /device:TPU:2 before, /device:TPU:16 now
where the time goes in v2:
time: 60.8 us; the launch traced here: 60.6 us
  Pallas kernels  56.8 us (93%)
  other arithmetic  3.15 us (5%)
  between operations  0.67 us (1%)
    pallas_call x1, Pallas kernels, local(): pl.pallas_call(functools.partial(step, n), out_shape=jax.ShapeDtypeStruct...  56.8 us
    convert_element_type x1, other arithmetic, local(): (wide + damping * residual / (1.0 + ridge_weight)).astype(jnp.bfloat16)  3.15 us

profile of v2, /device:TPU:16, one launch (start us, length us, event | category | flops | bytes accessed | tf_op | source)
XLA Modules:
  0.0 60.6 jit_solution(12699136199314228098)
XLA Ops:
  0.6 0.0 copy-start
  0.6 0.0 copy-start.1
  0.7 56.8 %shard_map.77 = f32[1536,256]{1,0:T(8,128)} custom-call(s32[1,4]{1,0:T(1,128)} %mask_ref.1, bf16[1536,128]{1,0:T(8,128)(2,1)} %points_ref.1, bf16[1536,256]{1,0:T(8,128)(2,1)} %weights_ref.1, s32[1,256]{1,0:T(1,128)} %leaf_index_ref.1, s32[4,1,256]{2,1,0:T(1,128)} %node_index_ref.1), custom_call_target="tpu_custom_call" | custom-call | tf_op jit(solution)/shard_map/pallas_call | solution.py:355
  57.4 0.0 copy-done
  57.4 0.0 copy-done.1
  57.5 3.1 %fusion.1 = (bf16[1536,256]{1,0:T(8,128)(2,1)}, f32[1536,256]{1,0:T(8,128)}) fusion(bf16[1536,256]{1,0:T(8,128)(2,1)S(1)} %copy-done, f32[1536,256]{1,0:T(8,128)} %shard_map.77, bf16[1536,256]{1,0:T(8,128)(2,1)S(1)} %copy-done.1), kind=kLoop, calls=%fused_computation.3 | loop fusion | flops 2752512 | bytes 5505024 | tf_op jit(solution)/shard_map/convert_element_type | solution.py:390
Async XLA Ops:
  0.6 56.8 %copy-start = (bf16[1536,256]{1,0:T(8,128)(2,1)S(1)}, bf16[1536,256]{1,0:T(8,128)(2,1)}, u32[]{:S(2)}) copy-start(bf16[1536,256]{1,0:T(8,128)(2,1)} %weights_ref.1) | copy-start | bytes 2359300
  0.6 56.8 %copy-start.1 = (bf16[1536,256]{1,0:T(8,128)(2,1)S(1)}, bf16[1536,256]{1,0:T(8,128)(2,1)}, u32[]{:S(2)}) copy-start(bf16[1536,256]{1,0:T(8,128)(2,1)} %param.8) | copy-start | bytes 2359300
